TPU v7x, 32 devices: a whole 2x2x4 slice. The times are simulated.
32 devices in a mesh: row: 4 (over x, core), col: 8 (over z, y).
Axes of the slice: x: 2, y: 2, z: 4, core: 2. Of those that a mesh axis runs over, the one named last changes fastest.
Arguments:
- corner: bfloat16 [25600, 25600], P('row', 'col'), may hold values from -32 to 32
- edge: bfloat16 [25600, 25600], P('row', 'col'), may hold values from -32 to 32
- sketch: bfloat16 [25600, 448], P('col'), may hold values from -6 to 6
Outputs:
- corner_new: float32 [400, 400], replicated
- edge_new: float32 [400, 400], replicated
All inputs are finite; a program needn't handle non-finite values.
Results may differ from a plain program's by a relative error of at most 0.0015.
Values may be sent and summed in bfloat16 or wider, within the bound.
A program may use at most 256 MiB of HBM per device.

v0:
```python
import jax
import jax.numpy as jnp
from jax import lax
from jax.sharding import PartitionSpec as P

RANK = 400
HIGHEST = lax.Precision.HIGHEST


def outer(left, right):
    return lax.dot_general(
        left, right, (((0,), (0,)), ((), ())), preferred_element_type=jnp.float32
    )


def exact_left(rows, image):
    upper_part = image.astype(jnp.bfloat16)
    lower_part = (image - upper_part.astype(jnp.float32)).astype(jnp.bfloat16)
    return outer(rows, upper_part) + outer(rows, lower_part)


def inverse_factor(gram):
    lower = jnp.linalg.cholesky(gram)
    unit = jnp.eye(gram.shape[0], dtype=gram.dtype)
    inverse = lax.linalg.triangular_solve(lower, unit, left_side=True, lower=True)
    return inverse[gram.shape[0] - RANK :]


def column_route(n_row, n_col):
    ratio = n_col // n_row
    route = []
    for source in range(n_row):
        for shard in range(n_col):
            half, target = divmod(shard, n_row)
            route.append((source * n_col + shard, target * n_col + source * ratio + half))
    return route


def body(corner, edge, sketch):
    n_row, n_col = (lax.axis_size("row"), lax.axis_size("col"))
    both = ("row", "col")
    part = jnp.dot(corner, sketch, preferred_element_type=jnp.float32).astype(jnp.bfloat16)
    shard = lax.psum_scatter(part, "col", scatter_dimension=0, tiled=True)
    gram = lax.psum(outer(shard, shard), both)
    moved = lax.ppermute(shard, both, column_route(n_row, n_col))
    cols = lax.all_gather(moved, "row", axis=0, tiled=True)
    rows = lax.all_gather(shard, "col", axis=0, tiled=True)
    inverse = inverse_factor(gram)

    def renormalize(matrix):
        image = jnp.dot(matrix, cols, preferred_element_type=jnp.float32)
        total = exact_left(rows, image)
        half = jnp.dot(inverse, total, precision=HIGHEST)
        return lax.dot_general(half, inverse, (((1,), (1,)), ((), ())), precision=HIGHEST)

    return lax.psum((renormalize(corner), renormalize(edge)), both)


def solution(mesh):
    placed = (P("row", "col"), P("row", "col"), P("col", None))
    return jax.shard_map(body, mesh=mesh, in_specs=placed, out_specs=(P(), P()), check_vma=False)
```

profile of v0, /device:TPU:0, one launch (start us, length us, event | category | flops | bytes accessed | tf_op | source)
XLA Modules:
  0.0 720.3 jit_solution(4127353241187174518)
XLA Ops:
  7.2 1.8 copy-done
  9.0 27.6 %convolution_convert_fusion = bf16[6400,448]{0,1:T(8,128)(2,1)} fusion(bf16[6400,3200]{1,0:T(8,128)(2,1)} %param.3, bf16[3200,448]{0,1:T(8,128)(2,1)S(1)} %copy-done), kind=kOutput, calls=%fused_computation.8 | convolution fusion | flops 18352947200 | bytes 49561600 | tf_op jit(solution)/shard_map/dot_general | solution.py:42
  36.5 9.2 %copy.22 = bf16[6400,448]{1,0:T(8,128)(2,1)} copy(bf16[6400,448]{0,1:T(8,128)(2,1)} %convolution_convert_fusion) | data formatting | bytes 11468800
  45.9 124.6 %reduce-scatter.4.cloned.1.call-done = bf16[800,448]{1,0:T(8,128)(2,1)} async-done(((bf16[6400,448]{1,0:T(8,128)(2,1)}), bf16[800,448]{1,0:T(8,128)(2,1)}) %reduce-scatter.4.cloned.1.call-update) | async-done | bytes 716816
  170.5 1.7 copy.23
  172.9 3.1 fusion.59
  176.1 0.9 copy-done.8
  177.9 137.3 %all-reduce.7.cloned.1.call-done = f32[448,448]{0,1:T(8,128)} async-done(((f32[448,448]{0,1:T(8,128)}), f32[448,448]{0,1:T(8,128)}) %all-reduce.7.cloned.1.call-update) | async-done | bytes 802832 | tf_op jit(solution)/shard_map/psum | solution.py:44
  315.1 1.5 copy.14
  316.6 1.4 fusion.14
  318.0 0.9 copy-done.7
  319.0 11.7 %cholesky.105 = f32[128,128]{1,0:T(8,128)S(1)} custom-call(f32[128,128]{1,0:T(8,128)S(1)} %cholesky.272), custom_call_target="Cholesky" | custom-call | tf_op jit(solution)/shard_map/jit(cholesky)/cholesky | solution.py:23
  330.8 9.8 %custom-call.30 = f32[1,128,128]{1,2,0:T(8,128)S(1)} custom-call(f32[1,128,128]{2,1,0:T(8,128)S(1)} %get-tuple-element.29), custom_call_target="InvertDiagBlocksLowerTriangular" | custom-call | tf_op jit(solution)/shard_map/jit(cholesky)/cholesky | solution.py:23
  340.6 1.2 constant_dynamic-update-slice_fusion.3
  341.8 1.2 convolution_subtract_fusion.3
  343.1 11.7 %cholesky.219 = f32[128,128]{1,0:T(8,128)S(1)} custom-call(f32[128,128]{1,0:T(8,128)S(1)} %cholesky.276), custom_call_target="Cholesky" | custom-call | tf_op jit(solution)/shard_map/jit(cholesky)/cholesky | solution.py:23
  354.8 10.2 %custom-call.31 = f32[1,128,128]{1,2,0:T(8,128)S(1)} custom-call(f32[1,128,128]{2,1,0:T(8,128)S(1)} %get-tuple-element.26), custom_call_target="InvertDiagBlocksLowerTriangular" | custom-call | tf_op jit(solution)/shard_map/jit(cholesky)/cholesky | solution.py:23
  365.3 1.2 convolution_subtract_fusion.4
  366.5 11.7 %cholesky.240 = f32[128,128]{1,0:T(8,128)S(1)} custom-call(f32[128,128]{1,0:T(8,128)S(1)} %cholesky.281), custom_call_target="Cholesky" | custom-call | tf_op jit(solution)/shard_map/jit(cholesky)/cholesky | solution.py:23
  378.2 9.8 %custom-call.32 = f32[1,128,128]{1,2,0:T(8,128)S(1)} custom-call(f32[1,128,128]{2,1,0:T(8,128)S(1)} %get-tuple-element.23), custom_call_target="InvertDiagBlocksLowerTriangular" | custom-call | tf_op jit(solution)/shard_map/jit(cholesky)/cholesky | solution.py:23
  388.3 1.0 convolution_subtract_fusion.5
  389.9 5.8 cholesky.260
  399.9 0.8 copy-done.6
  400.7 9.0 %while.1 = (s32[]{:T(128)}, f32[448,448]{1,0:T(8,128)}, s32[3,2]{0,1:T(2,128)S(1)}, f32[3,128,128]{2,1,0:T(8,128)S(1)}, s32[]{:T(128)}) while((s32[]{:T(128)}, f32[448,448]{1,0:T(8,128)}, s32[3,2]{0,1:T(2,128)S(1)}, f32[3,128,128]{2,1,0:T(8,128)S(1)}, s32[]{:T(128)}) %tuple.46), condition=%wide.while_cond, body=%wide.while_body.sunk | while | flops 2 | bytes 131189 | solution.py:25
  401.6 2.3 bitcast_dynamic-update-slice_fusion.2
  404.5 2.3 bitcast_dynamic-update-slice_fusion.2
  407.5 2.3 bitcast_dynamic-update-slice_fusion.2
  409.8 39.3 %custom-call.33 = f32[4,128,128]{1,2,0:T(8,128)S(1)} custom-call(f32[4,128,128]{2,1,0:T(8,128)S(1)} %pad_maximum_fusion.3), custom_call_target="InvertDiagBlocksLowerTriangular" | custom-call | tf_op jit(solution)/shard_map/triangular_solve | solution.py:25
  449.4 1.2 convolution_subtract_fusion.2
  450.9 1.4 convolution_subtract_fusion.1
  452.7 1.6 convolution_subtract_fusion
  454.7 6.2 copy.18
  460.9 6.3 reshape.63
  467.1 28.6 %fusion.60 = f32[448,6400]{1,0:T(8,128)} fusion(bf16[3200,448]{0,1:T(8,128)(2,1)} %reshape.63, bf16[6400,3200]{1,0:T(8,128)(2,1)} %param.3), kind=kOutput, calls=%fused_computation.100 | convolution fusion | flops 18350080000 | bytes 55296000 | tf_op jit(solution)/shard_map/dot_general | solution.py:51
  495.7 28.9 %fusion.61 = f32[448,6400]{1,0:T(8,128)} fusion(bf16[3200,448]{0,1:T(8,128)(2,1)} %reshape.63, bf16[6400,3200]{1,0:T(8,128)(2,1)} %param.4), kind=kOutput, calls=%fused_computation.101 | convolution fusion | flops 18350080000 | bytes 55296000 | tf_op jit(solution)/shard_map/dot_general | solution.py:51
  524.6 9.2 %copy.17 = bf16[8,800,448]{1,0,2:T(8,128)(2,1)} copy(bf16[8,800,448]{1,2,0:T(8,128)(2,1)} %all-gather.5.cloned.1.call-done) | data formatting | bytes 11468800 | tf_op jit(solution)/shard_map/all_gather | solution.py:47
  533.8 11.2 %reshape.61 = bf16[6400,448]{0,1:T(8,128)(2,1)} reshape(bf16[8,800,448]{1,0,2:T(8,128)(2,1)} %copy.17) | data formatting | bytes 11468800
  545.0 8.9 %fusion.55 = f32[448,448]{1,0:T(8,128)S(1)} fusion(bf16[6400,448]{0,1:T(8,128)(2,1)} %reshape.61, f32[448,6400]{1,0:T(8,128)} %fusion.60), kind=kOutput, calls=%fused_computation.97 | convolution fusion | flops 2569011200 | bytes 18006016 | tf_op jit(solution)/shard_map/dot_general | solution.py:11
  553.9 6.7 fusion.11
  560.6 2.5 fusion.48
  563.1 2.7 fusion.47
  565.8 3.1 fusion.53
  569.0 3.1 fusion.8
  572.2 2.5 fusion.46
  574.7 2.7 fusion.49
  577.4 131.7 %all-reduce.9.cloned.1.call-done = (f32[400,400]{1,0:T(8,128)}, f32[400,400]{1,0:T(8,128)}) async-done(((f32[400,400]{1,0:T(8,128)}, f32[400,400]{1,0:T(8,128)}), (f32[400,400]{1,0:T(8,128)}, f32[400,400]{1,0:T(8,128)})) %all-reduce.9.cloned.1.call-update) | async-done | bytes 1280016 | tf_op jit(solution)/shard_map/psum | solution.py:56
  709.1 2.1 copy.43
  711.2 2.1 copy.44
  (69 shorter events, 7.9 us)
Async XLA Ops:
  7.2 1.8 copy-start
  7.2 163.3 %reduce-scatter.4.cloned.1.call-start = ((), (), s32[]{:S(2)}) async-start(), calls=%async_computation.4 | async-start | bytes 7372800
  45.8 269.3 %all-reduce.7.cloned.1.call-start = ((), (), s32[]{:S(2)}) async-start(), calls=%async_computation.1 | async-start | bytes 1835008 | tf_op jit(solution)/shard_map/psum | solution.py:44
  172.2 5.1 copy-start.5
  172.2 3.9 collective-permute-start
  176.0 278.6 %all-gather.7.cloned.1.call-start = ((), (), s32[]{:S(2)}) async-start(), calls=%async_computation.3 | async-start | bytes 4014080 | tf_op jit(solution)/shard_map/all_gather | solution.py:46
  176.1 0.9 copy-start.8
  177.0 347.6 %all-gather.5.cloned.1.call-start = ((), (), s32[]{:S(2)}) async-start(), calls=%async_computation.2 | async-start | bytes 7225344 | tf_op jit(solution)/shard_map/all_gather | solution.py:47
  177.6 531.5 %all-reduce.9.cloned.1.call-start = ((), (), s32[]{:S(2)}) async-start(), calls=%async_computation.5 | async-start | bytes 3276800 | tf_op jit(solution)/shard_map/psum | solution.py:56
  318.0 0.9 copy-start.7
  399.8 0.9 copy-start.6
  454.7 108.5 %copy-start.2 = (f32[64,448]{0,1:T(8,128)}, f32[64,448]{0,1:T(8,128)S(1)}, u32[]{:S(2)}) copy-start(f32[64,448]{0,1:T(8,128)S(1)} %fusion.42) | copy-start | bytes 344068
  545.0 8.9 %copy-start.4 = (bf16[6400,448]{0,1:T(8,128)(2,1)S(1)}, bf16[6400,448]{0,1:T(8,128)(2,1)}, u32[]{:S(2)}) copy-start(bf16[6400,448]{0,1:T(8,128)(2,1)} %reshape.61) | copy-start | bytes 17203204
  545.0 20.8 %slice-start = ((s8[11468800]{0:T(1024)(128)(4,1)}), s8[4194304]{0:T(1024)(128)(4,1)S(1)}, s32[]{:S(2)}) async-start(s8[11468800]{0:T(1024)(128)(4,1)} %bitcast.121), calls=%async_computation.6 | async-start | bytes 8388608
  545.0 20.8 %slice-start.1 = ((s8[11468800]{0:T(1024)(128)(4,1)}), s8[4194304]{0:T(1024)(128)(4,1)S(1)}, s32[]{:S(2)}) async-start(s8[11468800]{0:T(1024)(128)(4,1)} %bitcast.121), calls=%async_computation.7 | async-start | bytes 8388608
  553.9 11.9 %slice-start.2 = ((s8[11468800]{0:T(1024)(128)(4,1)}), s8[3080192]{0:T(1024)(128)(4,1)S(1)}, s32[]{:S(2)}) async-start(s8[11468800]{0:T(1024)(128)(4,1)} %bitcast.121), calls=%async_computation.8 | async-start | bytes 6160384
  569.0 3.2 copy-start.3
  569.0 144.3 %copy-start.1 = (bf16[3200,448]{0,1:T(8,128)(2,1)S(1)}, bf16[3200,448]{0,1:T(8,128)(2,1)}, u32[]{:S(2)}) copy-start(bf16[3200,448]{0,1:T(8,128)(2,1)} %param.5) | copy-start | bytes 8601604
Sparse Core Ops, SparseCore 0:
  45.9 124.5 reduce-scatter.3
  176.2 138.9 all-reduce.6
  317.3 27.8 all-gather.6
  347.8 101.0 all-gather.4
  577.5 131.5 all-reduce.8
where the time goes:
time: 726 us; the launch traced here: 720 us
  waiting for transfers between devices  394 us (54%)
  matrix products  131 us (18%)
  other arithmetic  114 us (16%)
  local copies, waits for them, and re-layouts  62.8 us (9%)
  between operations  17.2 us (2%)
    psum x1, waiting for transfers between devices, body(): gram = lax.psum(outer(shard, shard), both)  137 us
    psum x1, waiting for transfers between devices, body(): return lax.psum((renormalize(corner), renormalize(edge)), both)  132 us
    unnamed x6, waiting for transfers between devices  125 us
    another operation x14, other arithmetic, inverse_factor(): lower = jnp.linalg.cholesky(gram)  72.9 us
    dot_general x2, matrix products, renormalize(): image = jnp.dot(matrix, cols, preferred_element_type=jnp.float32)  57.5 us
    another operation x7, other arithmetic, inverse_factor(): lax.linalg.triangular_solve(lower, unit, left_side=True, lower=True)  39.5 us
    unnamed x30, local copies, waits for them, and re-layouts  37.1 us
    dot_general x1, matrix products, body(): jnp.dot(corner, sketch, preferred_element_type=jnp.float32)  27.6 us
  transfers between devices with their start and end apart: 6, of which 3 were waited for; matrix products, arithmetic and copies ran while one was open for 29% of the time, Pallas kernels for 0%

commit v1 on v0

--- a/solution.py
+++ b/solution.py
@@ -41,7 +41,7 @@
     both = ("row", "col")
     part = jnp.dot(corner, sketch, preferred_element_type=jnp.float32).astype(jnp.bfloat16)
     shard = lax.psum_scatter(part, "col", scatter_dimension=0, tiled=True)
-    gram = lax.psum(outer(shard, shard), both)
+    gram = jnp.sum(lax.all_gather(outer(shard, shard), both), axis=0)
     moved = lax.ppermute(shard, both, column_route(n_row, n_col))
     cols = lax.all_gather(moved, "row", axis=0, tiled=True)
     rows = lax.all_gather(shard, "col", axis=0, tiled=True)

time: 726 us -> 823 us (1.13)
  waiting for transfers between devices: 394 us -> 480 us
  other arithmetic: 114 us -> 125 us
    psum x1 -> x0, waiting for transfers between devices: 137 us -> none  [body(): gram = lax.psum(outer(shard, shard), both)]
    all_gather x0 -> x1, waiting for transfers between devices: none -> 127 us  [body(): gram = jnp.sum(lax.all_gather(outer(shard, shard), both), axis=0)]
    all_gather x1, waiting for transfers between devices: 0.02 us -> 61.4 us  [body(): cols = lax.all_gather(moved, 'row', axis=0, tiled=True)]
    all_gather x1, waiting for transfers between devices: 0.01 us -> 35.7 us  [body(): rows = lax.all_gather(shard, 'col', axis=0, tiled=True)]
    reduce_sum x0 -> x1, other arithmetic: none -> 11.1 us  [body(): gram = jnp.sum(lax.all_gather(outer(shard, shard), both), axis=0)]
    unnamed x30 -> x26, local copies, waits for them, and re-layouts: 37.1 us -> 35.5 us
  transfers between devices with their start and end apart: 6 -> 6, of which waited for: 3 -> 5; matrix products, arithmetic and copies ran while one was open for 29% -> 15% of each run, Pallas kernels for 0% -> 0%
where the time goes in v1:
time: 823 us; the launch traced here: 815 us
  waiting for transfers between devices  480 us (58%)
  matrix products  135 us (16%)
  other arithmetic  125 us (15%)
  local copies, waits for them, and re-layouts  57.2 us (7%)
  between operations  17 us (2%)
    psum x1, waiting for transfers between devices, body(): return lax.psum((renormalize(corner), renormalize(edge)), both)  131 us
    all_gather x1, waiting for transfers between devices, body(): gram = jnp.sum(lax.all_gather(outer(shard, shard), both), axis=0)  127 us
    unnamed x6, waiting for transfers between devices  125 us
    another operation x14, other arithmetic, inverse_factor(): lower = jnp.linalg.cholesky(gram)  73 us
    all_gather x1, waiting for transfers between devices, body(): cols = lax.all_gather(moved, 'row', axis=0, tiled=True)  61.4 us
    dot_general x2, matrix products, renormalize(): image = jnp.dot(matrix, cols, preferred_element_type=jnp.float32)  55.9 us
    another operation x7, other arithmetic, inverse_factor(): lax.linalg.triangular_solve(lower, unit, left_side=True, lower=True)  39.7 us
    all_gather x1, waiting for transfers between devices, body(): rows = lax.all_gather(shard, 'col', axis=0, tiled=True)  35.7 us
  transfers between devices with their start and end apart: 6, of which 5 were waited for; matrix products, arithmetic and copies ran while one was open for 15% of the time, Pallas kernels for 0%

profile of v1, /device:TPU:0, one launch (start us, length us, event | category | flops | bytes accessed | tf_op | source)
XLA Modules:
  0.0 815.3 jit_solution(12398238981673407968)
XLA Ops:
  7.2 1.8 copy-done
  9.0 27.6 %convolution_convert_fusion = bf16[6400,448]{0,1:T(8,128)(2,1)} fusion(bf16[6400,3200]{1,0:T(8,128)(2,1)} %param.3, bf16[3200,448]{0,1:T(8,128)(2,1)S(1)} %copy-done), kind=kOutput, calls=%fused_computation.8 | convolution fusion | flops 18352947200 | bytes 49561600 | tf_op jit(solution)/shard_map/dot_general | solution.py:42
  36.6 9.1 %copy.18 = bf16[6400,448]{1,0:T(8,128)(2,1)} copy(bf16[6400,448]{0,1:T(8,128)(2,1)} %convolution_convert_fusion) | data formatting | bytes 11468800
  45.8 124.6 %reduce-scatter.4.cloned.1.call-done = bf16[800,448]{1,0:T(8,128)(2,1)} async-done(((bf16[6400,448]{1,0:T(8,128)(2,1)}), bf16[800,448]{1,0:T(8,128)(2,1)}) %reduce-scatter.4.cloned.1.call-update) | async-done | bytes 716816
  170.4 1.7 copy.19
  172.2 0.7 collective-permute-start
  172.9 0.9 copy-done.6
  174.6 3.0 fusion.59
  177.8 1.1 fusion.23
  178.9 61.4 %all-gather.11.cloned.1.call-done = bf16[4,800,448]{1,2,0:T(8,128)(2,1)} async-done(((bf16[1,800,448]{1,2,0:T(8,128)(2,1)}), bf16[4,800,448]{1,2,0:T(8,128)(2,1)}) %all-gather.11.cloned.1.call-update) | async-done | bytes 2867216 | tf_op jit(solution)/shard_map/all_gather | solution.py:46
  240.3 6.0 copy.15
  246.3 5.5 reshape.64
  251.8 28.0 %fusion.60 = f32[448,6400]{1,0:T(8,128)} fusion(bf16[3200,448]{0,1:T(8,128)(2,1)S(1)} %reshape.64, bf16[6400,3200]{1,0:T(8,128)(2,1)} %param.3), kind=kOutput, calls=%fused_computation.100 | convolution fusion | flops 18350080000 | bytes 55296000 | tf_op jit(solution)/shard_map/dot_general | solution.py:51
  279.9 27.8 %fusion.61 = f32[448,6400]{1,0:T(8,128)} fusion(bf16[3200,448]{0,1:T(8,128)(2,1)S(1)} %reshape.64, bf16[6400,3200]{1,0:T(8,128)(2,1)} %param.4), kind=kOutput, calls=%fused_computation.101 | convolution fusion | flops 18350080000 | bytes 55296000 | tf_op jit(solution)/shard_map/dot_general | solution.py:51
  307.7 35.7 %all-gather.9.cloned.1.call-done = bf16[8,800,448]{1,2,0:T(8,128)(2,1)} async-done(((bf16[1,800,448]{1,2,0:T(8,128)(2,1)}), bf16[8,800,448]{1,2,0:T(8,128)(2,1)}) %all-gather.9.cloned.1.call-update) | async-done | bytes 5734416 | tf_op jit(solution)/shard_map/all_gather | solution.py:47
  343.4 9.2 %copy.14 = bf16[8,800,448]{1,0,2:T(8,128)(2,1)} copy(bf16[8,800,448]{1,2,0:T(8,128)(2,1)} %all-gather.9.cloned.1.call-done) | data formatting | bytes 11468800 | tf_op jit(solution)/shard_map/all_gather | solution.py:47
  352.6 11.3 %reshape.62 = bf16[6400,448]{0,1:T(8,128)(2,1)} reshape(bf16[8,800,448]{1,0,2:T(8,128)(2,1)} %copy.14) | data formatting | bytes 11468800
  363.9 9.1 %fusion.53 = f32[448,448]{1,0:T(8,128)S(1)} fusion(bf16[6400,448]{0,1:T(8,128)(2,1)} %reshape.62, f32[448,6400]{1,0:T(8,128)} %fusion.61), kind=kOutput, calls=%fused_computation.95 | convolution fusion | flops 2569011200 | bytes 18006016 | tf_op jit(solution)/shard_map/dot_general | solution.py:11
  373.1 6.3 fusion.55
  379.4 8.0 fusion.8
  387.5 4.1 fusion.11
  391.6 126.9 %all-gather.7.cloned.1.call-done = f32[14336,448]{1,0:T(8,128)} async-done(((f32[448,448]{1,0:T(8,128)}), f32[14336,448]{1,0:T(8,128)}) %all-gather.7.cloned.1.call-update) | async-done | bytes 25690128 | tf_op jit(solution)/shard_map/all_gather | solution.py:44
  518.5 11.1 %reduce_sum.9 = f32[448,448]{1,0:T(8,128)S(1)} reduce(f32[32,448,448]{2,1,0:T(8,128)} %bitcast.120, f32[]{:T(128)} %constant.141.clone.1), dimensions={0}, to_apply=%region_1.0 | reduce | flops 6221824 | bytes 26492932 | tf_op jit(solution)/shard_map/reduce_sum | solution.py:44
  530.1 0.9 copy-done.5
  531.0 11.7 %cholesky.105 = f32[128,128]{1,0:T(8,128)S(1)} custom-call(f32[128,128]{1,0:T(8,128)S(1)} %cholesky.272), custom_call_target="Cholesky" | custom-call | tf_op jit(solution)/shard_map/jit(cholesky)/cholesky | solution.py:23
  542.9 9.8 %custom-call.30 = f32[1,128,128]{1,2,0:T(8,128)S(1)} custom-call(f32[1,128,128]{2,1,0:T(8,128)S(1)} %get-tuple-element.29), custom_call_target="InvertDiagBlocksLowerTriangular" | custom-call | tf_op jit(solution)/shard_map/jit(cholesky)/cholesky | solution.py:23
  552.7 1.2 constant_dynamic-update-slice_fusion.3
  553.9 1.2 convolution_subtract_fusion.3
  555.2 11.7 %cholesky.219 = f32[128,128]{1,0:T(8,128)S(1)} custom-call(f32[128,128]{1,0:T(8,128)S(1)} %cholesky.276), custom_call_target="Cholesky" | custom-call | tf_op jit(solution)/shard_map/jit(cholesky)/cholesky | solution.py:23
  566.9 10.2 %custom-call.31 = f32[1,128,128]{1,2,0:T(8,128)S(1)} custom-call(f32[1,128,128]{2,1,0:T(8,128)S(1)} %get-tuple-element.26), custom_call_target="InvertDiagBlocksLowerTriangular" | custom-call | tf_op jit(solution)/shard_map/jit(cholesky)/cholesky | solution.py:23
  577.4 1.2 convolution_subtract_fusion.4
  578.6 11.7 %cholesky.240 = f32[128,128]{1,0:T(8,128)S(1)} custom-call(f32[128,128]{1,0:T(8,128)S(1)} %cholesky.281), custom_call_target="Cholesky" | custom-call | tf_op jit(solution)/shard_map/jit(cholesky)/cholesky | solution.py:23
  591.0 9.8 %custom-call.32 = f32[1,128,128]{1,2,0:T(8,128)S(1)} custom-call(f32[1,128,128]{2,1,0:T(8,128)S(1)} %get-tuple-element.23), custom_call_target="InvertDiagBlocksLowerTriangular" | custom-call | tf_op jit(solution)/shard_map/jit(cholesky)/cholesky | solution.py:23
  601.1 1.0 convolution_subtract_fusion.5
  602.1 5.8 cholesky.260
  607.9 0.7 compare_reduce_fusion
  612.0 6.0 while.1
  612.6 1.4 bitcast_dynamic-update-slice_fusion.2
  614.6 1.4 bitcast_dynamic-update-slice_fusion.2
  616.6 1.4 bitcast_dynamic-update-slice_fusion.2
  618.2 39.5 %custom-call.33 = f32[4,128,128]{1,2,0:T(8,128)S(1)} custom-call(f32[4,128,128]{2,1,0:T(8,128)S(1)} %pad_maximum_fusion.3), custom_call_target="InvertDiagBlocksLowerTriangular" | custom-call | tf_op jit(solution)/shard_map/triangular_solve | solution.py:25
  660.6 3.8 fusion.46
  664.4 2.7 fusion.49
  667.1 3.7 fusion.48
  670.8 2.7 fusion.47
  673.5 130.9 %all-reduce.6.cloned.1.call-done = (f32[400,400]{1,0:T(8,128)}, f32[400,400]{1,0:T(8,128)}) async-done(((f32[400,400]{1,0:T(8,128)}, f32[400,400]{1,0:T(8,128)}), (f32[400,400]{1,0:T(8,128)}, f32[400,400]{1,0:T(8,128)})) %all-reduce.6.cloned.1.call-update) | async-done | bytes 1280016 | tf_op jit(solution)/shard_map/psum | solution.py:56
  804.4 2.1 copy.38
  806.5 2.1 copy.39
  (66 shorter events, 8.5 us)
Async XLA Ops:
  7.2 1.8 copy-start
  7.2 163.2 %reduce-scatter.4.cloned.1.call-start = ((), (), s32[]{:S(2)}) async-start(), calls=%async_computation.4 | async-start | bytes 7372800
  45.7 194.5 %all-gather.11.cloned.1.call-start = ((), (), s32[]{:S(2)}) async-start(), calls=%async_computation.3 | async-start | bytes 4014080 | tf_op jit(solution)/shard_map/all_gather | solution.py:46
  172.1 1.7 copy-start.3
  172.2 0.7 collective-permute-start
  172.9 0.9 copy-start.6
  173.8 169.6 %all-gather.9.cloned.1.call-start = ((), (), s32[]{:S(2)}) async-start(), calls=%async_computation.2 | async-start | bytes 7225344 | tf_op jit(solution)/shard_map/all_gather | solution.py:47
  174.5 343.9 %all-gather.7.cloned.1.call-start = ((), (), s32[]{:S(2)}) async-start(), calls=%async_computation.1 | async-start | bytes 30277632 | tf_op jit(solution)/shard_map/all_gather | solution.py:44
  177.6 626.8 %all-reduce.6.cloned.1.call-start = ((), (), s32[]{:S(2)}) async-start(), calls=%async_computation.5 | async-start | bytes 3276800 | tf_op jit(solution)/shard_map/psum | solution.py:56
  363.9 9.1 %copy-start.2 = (bf16[6400,448]{0,1:T(8,128)(2,1)S(1)}, bf16[6400,448]{0,1:T(8,128)(2,1)}, u32[]{:S(2)}) copy-start(bf16[6400,448]{0,1:T(8,128)(2,1)} %reshape.62) | copy-start | bytes 17203204
  373.1 14.3 %slice-start = ((s8[11468800]{0:T(1024)(128)(4,1)}), s8[4194304]{0:T(1024)(128)(4,1)S(1)}, s32[]{:S(2)}) async-start(s8[11468800]{0:T(1024)(128)(4,1)} %bitcast.123), calls=%async_computation.6 | async-start | bytes 8388608
  373.1 14.3 %slice-start.1 = ((s8[11468800]{0:T(1024)(128)(4,1)}), s8[4194304]{0:T(1024)(128)(4,1)S(1)}, s32[]{:S(2)}) async-start(s8[11468800]{0:T(1024)(128)(4,1)} %bitcast.123), calls=%async_computation.7 | async-start | bytes 8388608
  379.4 8.1 slice-start.2
  529.6 128.4 %copy-start.4 = (f32[448,448]{0,1:T(8,128)S(1)}, f32[448,448]{0,1:T(8,128)}, u32[]{:S(2)}) copy-start(f32[448,448]{0,1:T(8,128)} %fusion.23) | copy-start | bytes 2408452
  530.1 1.0 copy-start.5
  660.6 148.0 %copy-start.1 = (bf16[3200,448]{0,1:T(8,128)(2,1)S(1)}, bf16[3200,448]{0,1:T(8,128)(2,1)}, u32[]{:S(2)}) copy-start(bf16[3200,448]{0,1:T(8,128)(2,1)} %param.5) | copy-start | bytes 8601604
Sparse Core Ops, SparseCore 0:
  45.9 124.5 reduce-scatter.3
  173.9 66.3 all-gather.10
  243.0 100.2 all-gather.8
  346.1 172.2 all-gather.6
  673.6 130.7 all-reduce.5
